TPU v7x, 256 devices: a whole 4x4x8 slice. The times are simulated.
256 devices in a mesh: row: 16 (over z_lo, x, core), col: 16 (over z_hi, y).
Axes of the slice: x: 4, y: 4, z: 8 (z_hi: 4, z_lo: 2; z = z_hi * 2 + z_lo), core: 2. Of those that a mesh axis runs over, the one named last changes fastest.
Arguments:
- blocks_inverse: bfloat16 [12288, 12288], P('row', 'col'), as said below
- factor_rows: bfloat16 [2, 6144, 256], P(None, 'row'), may hold values from -0.15234375 to 0.15234375
- block_lists: int32 [2, 48], replicated, may hold values from 0 to 95, as said below
- diag_inverse: float32 [2, 256, 256], replicated, as said below
Outputs:
- column_inverse: float32 [2, 12288, 256], P(None, 'row')
- mirror_inverse: float32 [2, 256, 12288], P(None, None, 'col')
- diagonal_inverse: float32 [2, 256, 256], replicated
Inputs may be any that keep to these rules, and one draw needn't show every extreme that they name: blocks_inverse is exactly symmetric and positive definite. block_lists[s, m] is 2 * m or 2 * m + 1. diag_inverse[s] is symmetric.
All inputs are finite; a program needn't handle non-finite values.
Results may differ from a plain program's by a relative error of at most 0.0003.
Values may be sent and summed in bfloat16 or wider, within the bound.
A program may use at most 64 MiB of HBM per device.

v0:
```python
import jax
import jax.numpy as jnp
from jax import lax
from jax.sharding import PartitionSpec as P

BS = 128


def broadcast(x, axis, root):
    mine = lax.axis_index(axis) == root
    return lax.psum(jnp.where(mine, x, jnp.zeros_like(x)), axis)


def pair_bits(block_lists, first_block, block_count):
    local_lists = lax.dynamic_slice_in_dim(block_lists, first_block // 2, block_count // 2, 1)
    pair_first = 2 * (first_block // 2 + jnp.arange(block_count // 2, dtype=jnp.int32))
    return local_lists - pair_first[None, :]


def expand_pairs(packed, bits):
    sup_count = packed.shape[0]
    feature_count = packed.shape[2]
    pairs = bits.shape[1]
    grouped = packed.reshape(sup_count, pairs, 1, BS, feature_count)
    which = (
        bits[:, :, None, None, None] == jnp.arange(2, dtype=jnp.int32)[None, None, :, None, None]
    )
    dense = jnp.where(which, grouped, jnp.zeros((), packed.dtype))
    return dense.reshape(sup_count, pairs * 2 * BS, feature_count)


def compact_pairs(dense, bits):
    sup_count = dense.shape[0]
    feature_count = dense.shape[2]
    pairs = bits.shape[1]
    grouped = dense.reshape(sup_count, pairs, 2, BS, feature_count)
    chosen = jnp.where(bits[:, :, None, None] == 0, grouped[:, :, 0], grouped[:, :, 1])
    return chosen.reshape(sup_count, pairs * BS, feature_count)


def multiply_each(matrix, stacked):
    results = []
    for sup_index in range(stacked.shape[0]):
        results.append(
            jnp.dot(matrix, stacked[sup_index].astype(jnp.float32), precision=lax.Precision.HIGHEST)
        )
    return jnp.stack(results)


def local(blocks_inverse, factor_rows, block_lists, diag_inverse):
    row_index = lax.axis_index("row")
    col_index = lax.axis_index("col")
    row_blocks = blocks_inverse.shape[0] // BS
    col_blocks = blocks_inverse.shape[1] // BS
    row_bits = pair_bits(block_lists, row_index * row_blocks, row_blocks)
    col_bits = pair_bits(block_lists, col_index * col_blocks, col_blocks)
    packed_length = col_blocks // 2 * BS
    root_row = col_index * col_blocks // row_blocks
    gathered = lax.all_gather(factor_rows, "row", axis=1, tiled=True)
    column_packed = lax.dynamic_slice_in_dim(gathered, col_index * packed_length, packed_length, 1)
    column_dense = expand_pairs(column_packed, col_bits)
    blocks_wide = blocks_inverse.astype(jnp.float32)
    products = multiply_each(blocks_wide, column_dense)
    listed_products = compact_pairs(products, row_bits)
    diagonal_terms = jnp.einsum(
        "srw,srv->swv",
        factor_rows.astype(jnp.float32),
        listed_products,
        precision=lax.Precision.HIGHEST,
    )
    diagonal_inverse = diag_inverse + lax.psum(diagonal_terms, ("row", "col"))
    row_total = lax.psum(listed_products, "col")
    column_inverse = -expand_pairs(row_total, row_bits)
    mirror_total = broadcast(row_total, "row", root_row)
    mirror_inverse = jnp.transpose(-expand_pairs(mirror_total, col_bits), (0, 2, 1))
    return (column_inverse, mirror_inverse, diagonal_inverse)


def solution(mesh):
    return jax.shard_map(
        local,
        mesh=mesh,
        in_specs=(P("row", "col"), P(None, "row", None), P(), P()),
        out_specs=(P(None, "row", None), P(None, None, "col"), P()),
        check_vma=False,
    )
```

profile of v0, /device:TPU:1, one launch (start us, length us, event | category | flops | bytes accessed | tf_op | source)
XLA Modules:
  0.0 641.8 jit_solution(4474671392308871341)
XLA Ops:
  8.0 0.8 broadcast_compare_fusion
  8.8 0.8 dynamic-slice_subtract_fusion
  9.6 49.3 %all-gather.2.cloned.1.call-done = bf16[2,6144,256]{2,1,0:T(8,128)(2,1)} async-done(((bf16[2,384,256]{2,1,0:T(8,128)(2,1)}), bf16[2,6144,256]{2,1,0:T(8,128)(2,1)}) %all-gather.2.cloned.1.call-update) | async-done | bytes 6291472 | tf_op jit(solution)/shard_map/all_gather | solution.py:59
  59.0 1.0 constant_dynamic-slice_fusion
  60.1 0.8 fusion.1
  61.9 1.5 convolution_bitcast_fusion
  64.4 1.2 fusion
  65.6 1.0 copy.11
  66.6 1.0 copy.10
  67.8 3.0 convolution_bitcast_fusion.2
  72.3 160.2 %all-reduce.4.cloned.1.call-done = f32[2,384,256]{2,1,0:T(8,128)} async-done(((f32[2,384,256]{2,1,0:T(8,128)}), f32[2,384,256]{2,1,0:T(8,128)}) %all-reduce.4.cloned.1.call-update) | async-done | bytes 786448 | tf_op jit(solution)/shard_map/psum | solution.py:72
  232.5 0.9 broadcast_select_fusion.1
  234.0 267.5 %all-reduce.8.cloned.1.call-done = f32[2,256,256]{1,2,0:T(8,128)} async-done(((f32[2,256,256]{1,2,0:T(8,128)}), f32[2,256,256]{1,2,0:T(8,128)}) %all-reduce.8.cloned.1.call-update) | async-done | bytes 524304 | tf_op jit(solution)/shard_map/psum | solution.py:71
  501.5 1.1 add.48
  502.6 1.0 copy.17
  504.0 1.7 broadcast_in_dim.104
  505.7 2.5 broadcast_in_dim.105
  508.2 1.3 select_negate_fusion
  509.5 3.0 copy.16
  512.5 115.7 %all-reduce.6.cloned.1.call-done = f32[2,3,128,256]{3,2,1,0:T(8,128)} async-done(((f32[2,3,128,256]{3,2,1,0:T(8,128)}), f32[2,3,128,256]{3,2,1,0:T(8,128)}) %all-reduce.6.cloned.1.call-update) | async-done | bytes 786448 | tf_op jit(solution)/shard_map/psum | solution.py:11
  628.2 1.5 copy.13
  629.8 1.7 broadcast_in_dim.112
  631.4 2.5 broadcast_in_dim.113
  634.0 1.3 negate_bitcast_fusion
  (35 shorter events, 5.4 us)
Async XLA Ops:
  7.2 53.8 %copy-start = (bf16[768,768]{1,0:T(8,128)(2,1)S(1)}, bf16[768,768]{1,0:T(8,128)(2,1)}, u32[]{:S(2)}) copy-start(bf16[768,768]{1,0:T(8,128)(2,1)} %param.4) | copy-start | bytes 3538948
  7.2 51.8 %all-gather.2.cloned.1.call-start = ((), (), s32[]{:S(2)}) async-start(), calls=%async_computation | async-start | bytes 6684672 | tf_op jit(solution)/shard_map/all_gather | solution.py:59
  67.8 3.0 copy-start.1
  70.8 161.8 %all-reduce.4.cloned.1.call-start = ((), (), s32[]{:S(2)}) async-start(), calls=%async_computation.1 | async-start | bytes 1572864 | tf_op jit(solution)/shard_map/psum | solution.py:72
  71.5 162.3 %copy-start.3 = (f32[2,256,256]{2,1,0:T(8,128)S(1)}, f32[2,256,256]{2,1,0:T(8,128)}, u32[]{:S(2)}) copy-start(f32[2,256,256]{2,1,0:T(8,128)} %param.7) | copy-start | bytes 1572868
  71.5 430.0 %all-reduce.8.cloned.1.call-start = ((), (), s32[]{:S(2)}) async-start(), calls=%async_computation.3 | async-start | bytes 1048576 | tf_op jit(solution)/shard_map/psum | solution.py:71
  72.2 556.0 %all-reduce.6.cloned.1.call-start = ((), (), s32[]{:S(2)}) async-start(), calls=%async_computation.2 | async-start | bytes 1572864 | tf_op jit(solution)/shard_map/psum | solution.py:11
  234.0 269.6 %copy-start.2 = (f32[2,384,256]{2,1,0:T(8,128)S(1)}, f32[2,384,256]{2,1,0:T(8,128)}, u32[]{:S(2)}) copy-start(f32[2,384,256]{2,1,0:T(8,128)} %all-reduce.4.cloned.1.call-done) | copy-start | bytes 2359300
Sparse Core Ops, SparseCore 0:
  9.8 49.1 all-gather.1
  74.8 157.7 all-reduce.3
  238.6 262.8 all-reduce.7
  504.0 124.2 all-reduce.5
where the time goes:
time: 642 us
  waiting for transfers between devices  595 us (93%)
  local copies, waits for them, and re-layouts  21.3 us (3%)
  between operations  14 us (2%)
  other arithmetic  6.57 us (1%)
    psum x1, waiting for transfers between devices, local(): diagonal_inverse = diag_inverse + lax.psum(diagonal_terms, ('row', 'col'))  268 us
    psum x1, waiting for transfers between devices, local(): row_total = lax.psum(listed_products, 'col')  160 us
    psum x1, waiting for transfers between devices, broadcast(): return lax.psum(jnp.where(mine, x, jnp.zeros_like(x)), axis)  116 us
    all_gather x1, waiting for transfers between devices, local(): gathered = lax.all_gather(factor_rows, 'row', axis=1, tiled=True)  49.3 us
  transfers between devices with their start and end apart: 4, of which 4 were waited for; matrix products, arithmetic and copies ran while one was open for 2% of the time, Pallas kernels for 0%

commit v1 on v0

--- a/solution.py
+++ b/solution.py
@@ -56,7 +56,9 @@
     col_bits = pair_bits(block_lists, col_index * col_blocks, col_blocks)
     packed_length = col_blocks // 2 * BS
     root_row = col_index * col_blocks // row_blocks
-    gathered = lax.all_gather(factor_rows, "row", axis=1, tiled=True)
+    gathered = jnp.concatenate(
+        lax.all_to_all(jnp.stack([factor_rows] * lax.axis_size("row")), "row", 0, 0), axis=1
+    )
     column_packed = lax.dynamic_slice_in_dim(gathered, col_index * packed_length, packed_length, 1)
     column_dense = expand_pairs(column_packed, col_bits)
     blocks_wide = blocks_inverse.astype(jnp.float32)

time: 642 us -> 706 us (1.100)
  waiting for transfers between devices: 595 us -> 640 us
  local copies, waits for them, and re-layouts: 21.3 us -> 32.9 us
  starting transfers between devices: 0.12 us -> 7.95 us
    all_to_all x0 -> x1, waiting for transfers between devices: none -> 87.3 us  [local(): lax.all_to_all(jnp.stack([factor_rows] * lax.axis_size('row')), 'row', 0, 0)]
    all_gather x1 -> x0, waiting for transfers between devices: 49.3 us -> none  [local(): gathered = lax.all_gather(factor_rows, 'row', axis=1, tiled=True)]
    psum x1, waiting for transfers between devices: 160 us -> 168 us  [local(): row_total = lax.psum(listed_products, 'col')]
    all_to_all x0 -> x1, starting transfers between devices: none -> 7.7 us  [local(): lax.all_to_all(jnp.stack([factor_rows] * lax.axis_size('row')), 'row', 0, 0)]
where the time goes in v1:
time: 706 us; the launch traced here: 705 us
  waiting for transfers between devices  640 us (91%)
  local copies, waits for them, and re-layouts  32.9 us (5%)
  between operations  14 us (2%)
  starting transfers between devices  7.95 us (1%)
    psum x1, waiting for transfers between devices, local(): diagonal_inverse = diag_inverse + lax.psum(diagonal_terms, ('row', 'col'))  268 us
    psum x1, waiting for transfers between devices, local(): row_total = lax.psum(listed_products, 'col')  168 us
    psum x1, waiting for transfers between devices, broadcast(): return lax.psum(jnp.where(mine, x, jnp.zeros_like(x)), axis)  116 us
    all_to_all x1, waiting for transfers between devices, local(): lax.all_to_all(jnp.stack([factor_rows] * lax.axis_size('row')), 'row', 0, 0)  87.3 us
  transfers between devices with their start and end apart: 4, of which 4 were waited for; matrix products, arithmetic and copies ran while one was open for 2% of the time, Pallas kernels for 0%

profile of v1, /device:TPU:1, one launch (start us, length us, event | category | flops | bytes accessed | tf_op | source)
XLA Modules:
  0.0 705.2 jit_solution(3591739759308006651)
XLA Ops:
  7.2 4.4 stack.8
  11.6 7.7 %all-to-all-start = ((bf16[16,2,384,256]{3,2,1,0:T(8,128)(2,1)}), bf16[16,2,384,256]{3,2,1,0:T(8,128)(2,1)}, u32[]{:S(2)}, u32[]{:S(2)}) async-start(bf16[16,2,384,256]{3,2,1,0:T(8,128)(2,1)} %stack.8), calls=%async_computation | async-start | bytes 12582912 | tf_op jit(solution)/shard_map/all_to_all | solution.py:60
  19.7 87.3 %all-to-all-done = bf16[16,2,384,256]{3,2,1,0:T(8,128)(2,1)} async-done(((bf16[16,2,384,256]{3,2,1,0:T(8,128)(2,1)}), bf16[16,2,384,256]{3,2,1,0:T(8,128)(2,1)}, u32[]{:S(2)}, u32[]{:S(2)}) %all-to-all-start) | async-done | bytes 6291488 | tf_op jit(solution)/shard_map/all_to_all | solution.py:60
  106.9 3.2 copy.26
  113.0 1.4 convolution_bitcast_fusion
  114.4 1.5 stack.10
  116.3 2.1 fusion
  118.4 2.2 copy.27
  120.6 2.1 copy.28
  122.6 1.3 broadcast_select_fusion.2
  124.0 1.7 convolution_bitcast_fusion.2
  127.4 168.4 %all-reduce.4.cloned.1.call-done = f32[2,384,256]{2,1,0:T(8,128)} async-done(((f32[2,384,256]{2,1,0:T(8,128)}), f32[2,384,256]{2,1,0:T(8,128)}) %all-reduce.4.cloned.1.call-update) | async-done | bytes 786448 | tf_op jit(solution)/shard_map/psum | solution.py:74
  297.2 267.5 %all-reduce.8.cloned.1.call-done = f32[2,256,256]{1,2,0:T(8,128)} async-done(((f32[2,256,256]{1,2,0:T(8,128)}), f32[2,256,256]{1,2,0:T(8,128)}) %all-reduce.8.cloned.1.call-update) | async-done | bytes 524304 | tf_op jit(solution)/shard_map/psum | solution.py:73
  564.8 1.1 add.48
  565.9 1.0 copy.34
  567.2 1.7 broadcast_in_dim.104
  568.9 2.5 broadcast_in_dim.105
  571.5 1.3 select_negate_fusion
  572.8 3.0 copy.33
  575.8 115.9 %all-reduce.6.cloned.1.call-done = f32[2,3,128,256]{3,2,1,0:T(8,128)} async-done(((f32[2,3,128,256]{3,2,1,0:T(8,128)}), f32[2,3,128,256]{3,2,1,0:T(8,128)}) %all-reduce.6.cloned.1.call-update) | async-done | bytes 786448 | tf_op jit(solution)/shard_map/psum | solution.py:11
  691.7 1.5 copy.30
  693.2 1.7 broadcast_in_dim.112
  694.9 2.5 broadcast_in_dim.113
  697.4 1.3 negate_bitcast_fusion
  (42 shorter events, 7.0 us)
Async XLA Ops:
  7.2 103.9 %copy-start = (bf16[768,768]{1,0:T(8,128)(2,1)S(1)}, bf16[768,768]{1,0:T(8,128)(2,1)}, u32[]{:S(2)}) copy-start(bf16[768,768]{1,0:T(8,128)(2,1)} %param.4) | copy-start | bytes 3538948
  11.6 7.7 %copy-start.6 = (s32[2,48]{1,0:T(2,128)S(1)}, s32[2,48]{1,0:T(2,128)}, u32[]{:S(2)}) copy-start(s32[2,48]{1,0:T(2,128)} %param.6) | copy-start | bytes 1156
  11.6 95.3 %all-to-all-start = ((bf16[16,2,384,256]{3,2,1,0:T(8,128)(2,1)}), bf16[16,2,384,256]{3,2,1,0:T(8,128)(2,1)}, u32[]{:S(2)}, u32[]{:S(2)}) async-start(bf16[16,2,384,256]{3,2,1,0:T(8,128)(2,1)} %stack.8), calls=%async_computation | async-start | bytes 12582912 | tf_op jit(solution)/shard_map/all_to_all | solution.py:60
  112.0 1.0 copy-start.3
  122.6 1.4 copy-start.4
  124.0 1.7 copy-start.1
  125.7 170.1 %all-reduce.4.cloned.1.call-start = ((), (), s32[]{:S(2)}) async-start(), calls=%async_computation.1 | async-start | bytes 1572864 | tf_op jit(solution)/shard_map/psum | solution.py:74
  126.4 170.6 %copy-start.5 = (f32[2,256,256]{2,1,0:T(8,128)S(1)}, f32[2,256,256]{2,1,0:T(8,128)}, u32[]{:S(2)}) copy-start(f32[2,256,256]{2,1,0:T(8,128)} %param.7) | copy-start | bytes 1572868
  126.4 438.3 %all-reduce.8.cloned.1.call-start = ((), (), s32[]{:S(2)}) async-start(), calls=%async_computation.3 | async-start | bytes 1048576 | tf_op jit(solution)/shard_map/psum | solution.py:73
  127.2 564.5 %all-reduce.6.cloned.1.call-start = ((), (), s32[]{:S(2)}) async-start(), calls=%async_computation.2 | async-start | bytes 1572864 | tf_op jit(solution)/shard_map/psum | solution.py:11
  297.2 269.6 %copy-start.2 = (f32[2,384,256]{2,1,0:T(8,128)S(1)}, f32[2,384,256]{2,1,0:T(8,128)}, u32[]{:S(2)}) copy-start(f32[2,384,256]{2,1,0:T(8,128)} %all-reduce.4.cloned.1.call-done) | copy-start | bytes 2359300
Sparse Core Ops, SparseCore 0:
  129.7 166.0 all-reduce.3
  301.8 262.8 all-reduce.7
  567.4 124.2 all-reduce.5
